TPU v7x, 256 devices: a whole 4x4x8 slice. The times are simulated.
256 devices in a mesh: seq: 64 (over x, z, core), ch: 4 (over y).
Axes of the slice: x: 4, y: 4, z: 8, core: 2. Of those that a mesh axis runs over, the one named last changes fastest.
Arguments:
- proj: bfloat16 [3, 128, 65536], P(None, 'ch', 'seq'), may hold values from -6 to 6
- cotangent: bfloat16 [128, 65536], P('ch', 'seq'), may hold values from -6 to 6
- short_w: float32 [3, 128, 3], P(None, 'ch'), may hold values from -3.5 to 3.5
- filter_in: float32 [32, 64], replicated, may hold values from -5 to 5
- filter_out: float32 [64, 128], P(None, 'ch'), may hold values from -0.75 to 0.75
- rates: float32 [128], P('ch'), may hold values from 0.25 to 2184
Outputs:
- grad_proj: bfloat16 [3, 128, 65536], P(None, 'ch', 'seq')
- grad_short: float32 [3, 128, 3], P(None, 'ch')
- grad_filter_out: float32 [64, 128], P(None, 'ch')
- grad_filter_in: float32 [32, 64], replicated
All inputs are finite; a program needn't handle non-finite values.
Results may differ from a plain program's by a relative error of at most 0.0013.
Values may be sent and summed in bfloat16 or wider, within the bound.
A program may use at most 64 MiB of HBM per device.

v0:
```python
import math
import jax
import jax.numpy as jnp
from jax import lax
from jax.sharding import PartitionSpec as P

PRECISE = lax.Precision.HIGHEST


def shifted(value, axis, by):
    length = lax.axis_size(axis)
    pairs = [(i, i + by) for i in range(length) if 0 <= i + by < length]
    return lax.ppermute(value, axis, pairs)


def position_features(positions, length, feature_count):
    feature_index = jnp.arange(feature_count, dtype=jnp.int32)
    multiplier = (1 + feature_index // 2 * 499) % length
    upper = positions // 1024
    lower = positions % 1024
    phases = (
        upper[:, None] * (multiplier * 1024 % length)[None, :]
        + lower[:, None] * multiplier[None, :]
    ) % length
    angles = phases.astype(jnp.float32) * (2.0 * math.pi / length)
    return jnp.where((feature_index % 2 == 0)[None, :], jnp.cos(angles), jnp.sin(angles))


def angle_tables(row_count, col_count, row_start, col_start, modulus):
    row_index = row_start + jnp.arange(row_count, dtype=jnp.int32)
    col_index = col_start + jnp.arange(col_count, dtype=jnp.int32)
    phases = row_index[:, None] * col_index[None, :] % modulus
    angles = phases.astype(jnp.float32) * (2.0 * math.pi / modulus)
    return (jnp.cos(angles), jnp.sin(angles))


def rotate(real_part, imag_part, cosine, sine, sign):
    return (
        real_part * cosine - sign * imag_part * sine,
        imag_part * cosine + sign * real_part * sine,
    )


def dft_axis(real_part, imag_part, form, cosine, sine, sign):
    real_cos = jnp.einsum(form, real_part, cosine, precision=PRECISE)
    real_sin = jnp.einsum(form, real_part, sine, precision=PRECISE)
    imag_cos = jnp.einsum(form, imag_part, cosine, precision=PRECISE)
    imag_sin = jnp.einsum(form, imag_part, sine, precision=PRECISE)
    return (real_cos - sign * imag_sin, imag_cos + sign * real_sin)


def shards(proj, cotangent, short_w, filter_in, filter_out, rates):
    tap_count = short_w.shape[2]
    channels = proj.shape[1]
    devices = lax.axis_size("seq")
    tokens_here = proj.shape[2]
    length = devices * tokens_here
    modulus = 2 * length
    norm_scale = 1.0 / math.sqrt(length)
    column_width = tokens_here // devices
    first_split = math.gcd(tokens_here, 64)
    second_split = tokens_here // first_split
    device_index = lax.axis_index("seq")
    rim_cols = shifted(proj[:, :, tokens_here - (tap_count - 1) :], "seq", 1)
    extended = jnp.concatenate([rim_cols, proj], 2).astype(jnp.float32)

    def delayed(offset):
        return extended[:, :, tap_count - 1 - offset : tap_count - 1 - offset + tokens_here]

    mixed_all = short_w[:, :, 0, None] * delayed(0)
    for offset in range(1, tap_count):
        mixed_all = mixed_all + short_w[:, :, offset, None] * delayed(offset)
    query_part, key_part, value_part = (mixed_all[0], mixed_all[1], mixed_all[2])
    gated_prod = key_part * value_part
    cotangent_full = cotangent.astype(jnp.float32)
    grad_conv = cotangent_full * query_part
    both_signals = jnp.concatenate([gated_prod, grad_conv], 0).reshape(2 * channels, 1, tokens_here)
    columns = lax.all_to_all(both_signals, "seq", split_axis=2, concat_axis=1, tiled=True)
    block_start = jnp.arange(devices, dtype=jnp.int32) * tokens_here
    offset_start = device_index * column_width + jnp.arange(column_width, dtype=jnp.int32)
    column_pos = (block_start[:, None] + offset_start[None, :]).reshape(devices * column_width)
    features = position_features(column_pos, length, filter_in.shape[0])
    preact = jnp.dot(features, filter_in, precision=PRECISE, preferred_element_type=jnp.float32)
    hidden = jnp.sin(preact)
    modulated = jnp.einsum("to,oc->ct", hidden, filter_out, precision=PRECISE)
    relative = column_pos.astype(jnp.float32) / length
    spread = jnp.sqrt(jnp.expm1(-2.0 * rates) / jnp.expm1(-2.0 * rates / length))
    envelope = jnp.exp(-rates[:, None] * relative[None, :]) / spread[:, None]
    kernel = (envelope * modulated).reshape(channels, devices, column_width)
    stacked = jnp.concatenate([columns[:channels], kernel, columns[channels:]], 0)
    cos_outer, sin_outer = angle_tables(devices, 2 * devices, 0, 0, 2 * devices)
    turned_real = jnp.einsum("ran,ak->rkn", stacked, cos_outer, precision=PRECISE)
    turned_imag = -jnp.einsum("ran,ak->rkn", stacked, sin_outer, precision=PRECISE)
    cos_turn, sin_turn = angle_tables(
        2 * devices, column_width, 0, device_index * column_width, modulus
    )
    turned_real, turned_imag = rotate(turned_real, turned_imag, cos_turn, sin_turn, -1.0)
    moved_real, moved_imag = (
        lax.all_to_all(turned_real, "seq", split_axis=1, concat_axis=2, tiled=True),
        lax.all_to_all(turned_imag, "seq", split_axis=1, concat_axis=2, tiled=True),
    )
    row_total = moved_real.shape[0]
    cos_first, sin_first = angle_tables(first_split, first_split, 0, 0, first_split)
    cos_second, sin_second = angle_tables(second_split, second_split, 0, 0, second_split)
    cos_mid, sin_mid = angle_tables(first_split, second_split, 0, 0, tokens_here)
    grid_real = moved_real.reshape(row_total, 2, first_split, second_split)
    grid_imag = moved_imag.reshape(row_total, 2, first_split, second_split)
    grid_real, grid_imag = dft_axis(
        grid_real, grid_imag, "rkab,ac->rkcb", cos_first, sin_first, -1.0
    )
    grid_real, grid_imag = rotate(grid_real, grid_imag, cos_mid, sin_mid, -1.0)
    spec_real, spec_imag = dft_axis(
        grid_real, grid_imag, "rkcb,bd->rkcd", cos_second, sin_second, -1.0
    )
    gated_real, gated_imag = (spec_real[:channels], spec_imag[:channels])
    kernel_real, kernel_imag = (
        spec_real[channels : 2 * channels],
        spec_imag[channels : 2 * channels],
    )
    grad_real, grad_imag = (spec_real[2 * channels :], spec_imag[2 * channels :])
    conv_real = gated_real * kernel_real - gated_imag * kernel_imag
    conv_imag = gated_real * kernel_imag + gated_imag * kernel_real
    back_real = grad_real * kernel_real + grad_imag * kernel_imag
    back_imag = grad_imag * kernel_real - grad_real * kernel_imag
    kgrad_real = grad_real * gated_real + grad_imag * gated_imag
    kgrad_imag = grad_imag * gated_real - grad_real * gated_imag
    cos_back, sin_back = angle_tables(2, tokens_here, 2 * device_index, 0, modulus)
    cos_last, sin_last = angle_tables(2 * devices, devices, 0, 0, 2 * devices)
    real_part = jnp.concatenate([conv_real, back_real, kgrad_real], 0)
    rows = real_part.shape[0]
    part_real, part_imag = dft_axis(
        real_part,
        jnp.concatenate([conv_imag, back_imag, kgrad_imag], 0),
        "rkcd,db->rkcb",
        cos_second,
        sin_second,
        1.0,
    )
    part_real, part_imag = rotate(part_real, part_imag, cos_mid, sin_mid, 1.0)
    part_real, part_imag = dft_axis(
        part_real, part_imag, "rkcb,ca->rkab", cos_first, sin_first, 1.0
    )
    part_real = part_real.reshape(rows, 2, tokens_here)
    part_imag = part_imag.reshape(rows, 2, tokens_here)
    part_real, part_imag = rotate(part_real, part_imag, cos_back[None], sin_back[None], 1.0)
    spread_real = lax.all_to_all(part_real, "seq", split_axis=2, concat_axis=1, tiled=True)
    spread_imag = lax.all_to_all(part_imag, "seq", split_axis=2, concat_axis=1, tiled=True)
    real_out = jnp.einsum("rkn,ka->ran", spread_real, cos_last, precision=PRECISE)
    real_out = (real_out - jnp.einsum("rkn,ka->ran", spread_imag, sin_last, precision=PRECISE)) * (
        1.0 / modulus
    )
    conv_cols = real_out[:channels]
    gated_cols = real_out[channels : 2 * channels]
    kernel_grad = real_out[2 * channels :]
    returned = lax.all_to_all(
        jnp.concatenate([conv_cols, gated_cols], 0), "seq", split_axis=1, concat_axis=2, tiled=True
    )
    returned = returned.reshape(2 * channels, tokens_here)
    conv_out = returned[:channels]
    grad_gated = returned[channels:]
    grad_mixed = jnp.stack(
        [cotangent_full * conv_out, grad_gated * value_part, grad_gated * key_part]
    )
    short_part = jnp.stack(
        [jnp.sum(grad_mixed * delayed(offset), axis=2) for offset in range(tap_count)], axis=2
    )
    weighted = envelope * kernel_grad.reshape(channels, devices * column_width)
    out_part = jnp.einsum("to,ct->oc", hidden, weighted, precision=PRECISE)
    grad_hidden = jnp.einsum("ct,oc->to", weighted, filter_out, precision=PRECISE)
    in_part = jnp.einsum("tf,to->fo", features, grad_hidden * jnp.cos(preact), precision=PRECISE)
    next_rim = shifted(grad_mixed[:, :, : tap_count - 1], "seq", -1)
    grad_extended = jnp.concatenate([grad_mixed, next_rim], 2)
    result = short_w[:, :, 0, None] * grad_extended[:, :, 0:tokens_here]
    for offset in range(1, tap_count):
        result = (
            result
            + short_w[:, :, offset, None] * grad_extended[:, :, offset : offset + tokens_here]
        )
    grad_proj = result.astype(jnp.bfloat16)
    short_total, out_total = lax.psum((short_part, out_part), "seq")
    in_total = lax.psum(in_part, ("seq", "ch"))
    return (grad_proj, short_total * norm_scale, out_total * norm_scale, in_total * norm_scale)


def solution(mesh):
    placed = (
        P(None, "ch", "seq"),
        P("ch", "seq"),
        P(None, "ch", None),
        P(),
        P(None, "ch"),
        P("ch"),
    )
    return jax.shard_map(
        shards,
        mesh=mesh,
        in_specs=placed,
        out_specs=(P(None, "ch", "seq"), P(None, "ch", None), P(None, "ch"), P()),
        check_vma=False,
    )
```

profile of v0, /device:TPU:8, one launch (start us, length us, event | category | flops | bytes accessed | tf_op | source)
XLA Modules:
  0.0 598.5 jit_solution(10087766709720511439)
XLA Ops:
  1.5 1.7 collective-permute-start
  4.3 5.1 fusion.244
  12.4 3.8 reduce
  16.2 2.1 reshape.320
  18.3 13.3 %all-to-all-start = ((f32[64,1,1024]{2,1,0:T(1,128)}), f32[64,1,1024]{2,1,0:T(1,128)}, u32[]{:S(2)}, u32[]{:S(2)}) async-start(f32[64,1,1024]{2,1,0:T(1,128)} %reshape.320), calls=%async_computation | async-start | bytes 524288 | tf_op jit(solution)/shard_map/all_to_all | solution.py:78
  31.6 1.9 fusion.11
  33.5 1.9 copy.146
  35.4 2.0 copy.148
  37.6 5.8 all-to-all-done
  43.4 2.9 reduce.1
  46.4 2.4 reshape.321
  48.8 2.3 fusion.241
  52.2 1.7 convolution_negate_fusion
  53.9 2.9 add_bitcast_fusion.1
  56.9 2.5 copy.152
  59.4 6.3 %all-to-all-start.2 = ((f32[96,128,16]{0,2,1:T(8,128)}), f32[96,128,16]{0,2,1:T(8,128)}, u32[]{:S(2)}, u32[]{:S(2)}) async-start(f32[96,128,16]{0,2,1:T(8,128)} %copy.152), calls=%async_computation.2 | async-start | bytes 2097152 | tf_op jit(solution)/shard_map/all_to_all | solution.py:100
  65.6 2.5 copy.150
  68.2 25.5 %all-to-all-done.2 = f32[96,128,16]{0,2,1:T(8,128)} async-done(((f32[96,128,16]{0,2,1:T(8,128)}), f32[96,128,16]{0,2,1:T(8,128)}, u32[]{:S(2)}, u32[]{:S(2)}) %all-to-all-start.2) | async-done | bytes 786464 | tf_op jit(solution)/shard_map/all_to_all | solution.py:100
  93.7 7.2 %all-to-all-start.1 = ((f32[96,128,16]{0,2,1:T(8,128)}), f32[96,128,16]{0,2,1:T(8,128)}, u32[]{:S(2)}, u32[]{:S(2)}) async-start(f32[96,128,16]{0,2,1:T(8,128)} %copy.150), calls=%async_computation.1 | async-start | bytes 2097152 | tf_op jit(solution)/shard_map/all_to_all | solution.py:99
  101.4 3.8 fusion.14
  105.3 23.3 %all-to-all-done.1 = f32[96,128,16]{0,2,1:T(8,128)} async-done(((f32[96,128,16]{0,2,1:T(8,128)}), f32[96,128,16]{0,2,1:T(8,128)}, u32[]{:S(2)}, u32[]{:S(2)}) %all-to-all-start.1) | async-done | bytes 786464 | tf_op jit(solution)/shard_map/all_to_all | solution.py:99
  128.5 2.9 fusion.18
  131.5 2.9 fusion.7
  134.4 3.4 subtract_bitcast_fusion
  137.8 1.6 fusion.29
  139.4 1.6 fusion.33
  141.0 1.7 fusion.5
  142.7 1.8 fusion.6
  151.2 1.9 multiply_subtract_fusion
  154.5 1.6 fusion.27
  160.1 1.7 fusion.13
  161.8 1.8 copy.166
  163.5 6.8 %all-to-all-start.3 = ((f32[96,2,1024]{0,1,2:T(2,128)}), f32[96,2,1024]{0,1,2:T(2,128)}, u32[]{:S(2)}, u32[]{:S(2)}) async-start(f32[96,2,1024]{0,1,2:T(2,128)} %copy.166), calls=%async_computation.3 | async-start | bytes 2097152 | tf_op jit(solution)/shard_map/all_to_all | solution.py:146
  170.4 3.0 copy.170
  173.4 25.0 %all-to-all-done.3 = f32[96,2,1024]{0,1,2:T(2,128)} async-done(((f32[96,2,1024]{0,1,2:T(2,128)}), f32[96,2,1024]{0,1,2:T(2,128)}, u32[]{:S(2)}, u32[]{:S(2)}) %all-to-all-start.3) | async-done | bytes 786464 | tf_op jit(solution)/shard_map/all_to_all | solution.py:146
  198.4 6.8 %all-to-all-start.4 = ((f32[96,2,1024]{0,1,2:T(2,128)}), f32[96,2,1024]{0,1,2:T(2,128)}, u32[]{:S(2)}, u32[]{:S(2)}) async-start(f32[96,2,1024]{0,1,2:T(2,128)} %copy.170), calls=%async_computation.4 | async-start | bytes 2097152 | tf_op jit(solution)/shard_map/all_to_all | solution.py:147
  206.7 1.8 fusion.21
  208.5 24.7 %all-to-all-done.4 = f32[96,2,1024]{0,1,2:T(2,128)} async-done(((f32[96,2,1024]{0,1,2:T(2,128)}), f32[96,2,1024]{0,1,2:T(2,128)}, u32[]{:S(2)}, u32[]{:S(2)}) %all-to-all-start.4) | async-done | bytes 786464 | tf_op jit(solution)/shard_map/all_to_all | solution.py:147
  238.8 2.1 reshape.322
  240.9 7.0 %all-to-all-start.5 = ((f32[64,1,1024]{2,1,0:T(1,128)}), f32[64,1,1024]{2,1,0:T(1,128)}, u32[]{:S(2)}, u32[]{:S(2)}) async-start(f32[64,1,1024]{2,1,0:T(1,128)} %reshape.322), calls=%async_computation.5 | async-start | bytes 524288 | tf_op jit(solution)/shard_map/all_to_all | solution.py:155
  247.8 2.2 copy.175
  250.0 1.9 copy.176
  251.9 2.2 convolution_multiply_fusion.4
  254.1 3.0 fusion.43
  257.1 75.9 %psum.23 = f32[32,64]{1,0:T(8,128)S(1)} all-reduce(f32[32,64]{1,0:T(8,128)S(1)} %fusion.43), channel_id=1, replica_groups=mesh['seq'=64,'ch'=4] {'seq','ch'}, use_global_device_ids=true, to_apply=%region_5.6 | all-reduce | flops 2048 | bytes 16384 | tf_op jit(solution)/shard_map/psum | solution.py:181
  334.4 2.9 reduce.2
  337.4 1.9 reshape.323
  346.4 250.5 %all-reduce = (f32[3,32,3]{1,0,2:T(4,128)S(1)}, f32[64,32]{0,1:T(8,128)S(1)}) all-reduce(f32[3,32,3]{1,0,2:T(4,128)S(1)} %pad_maximum_fusion.7, f32[64,32]{0,1:T(8,128)S(1)} %fusion.238), channel_id=1, replica_groups=mesh['seq'=64,'ch'=4] {'seq'}, use_global_device_ids=true, to_apply=%region_3.4 | all-reduce | flops 2336 | bytes 18688 | tf_op jit(solution)/shard_map/psum | solution.py:180
  (94 shorter events, 35.0 us)
Async XLA Ops:
  0.6 3.7 copy-start
  0.6 8.8 %copy-start.6 = (bf16[32,1024]{1,0:T(8,128)(2,1)S(1)}, bf16[32,1024]{1,0:T(8,128)(2,1)}, u32[]{:S(2)}) copy-start(bf16[32,1024]{1,0:T(8,128)(2,1)} %param.7) | copy-start | bytes 196612
  1.5 8.1 %collective-permute-start = (bf16[3,32,2]{2,1,0:T(8,128)(2,1)S(1)}, bf16[3,32,2]{2,1,0:T(8,128)(2,1)S(1)}, u32[]{:S(2)}, u32[]{:S(2)}) collective-permute-start(bf16[3,32,2]{2,1,0:T(8,128)(2,1)S(1)} %slice.96), channel_id=1, source_target_pairs={{0,4},{4,8},{8,12},{12,16},{16,20},{20,24},{24,28},{28,32},{32,36}... | collective-permute-start | bytes 1160 | tf_op jit(solution)/shard_map/ppermute | solution.py:13
  3.3 6.3 %copy-start.10 = (s32[32]{0:T(128)}, s32[32]{0:T(128)S(1)}, u32[]{:S(2)}) copy-start(s32[32]{0:T(128)S(1)} %get-tuple-element.66) | copy-start | bytes 388
  3.3 6.3 %copy-start.12 = (pred[32]{0:T(512)(128)(4,1)}, pred[32]{0:T(512)(128)(4,1)S(1)}, u32[]{:S(2)}) copy-start(pred[32]{0:T(512)(128)(4,1)S(1)} %fusion.143) | copy-start | bytes 100
  4.3 5.3 copy-start.5
  11.9 19.7 %copy-start.9 = (f32[32]{0:T(128)S(1)}, f32[32]{0:T(128)}, u32[]{:S(2)}) copy-start(f32[32]{0:T(128)} %param.11) | copy-start | bytes 388
  11.9 19.7 %copy-start.7 = (f32[64,32]{0,1:T(8,128)S(1)}, f32[64,32]{0,1:T(8,128)}, u32[]{:S(2)}) copy-start(f32[64,32]{0,1:T(8,128)} %param.10) | copy-start | bytes 24580
  18.3 25.2 %all-to-all-start = ((f32[64,1,1024]{2,1,0:T(1,128)}), f32[64,1,1024]{2,1,0:T(1,128)}, u32[]{:S(2)}, u32[]{:S(2)}) async-start(f32[64,1,1024]{2,1,0:T(1,128)} %reshape.320), calls=%async_computation | async-start | bytes 524288 | tf_op jit(solution)/shard_map/all_to_all | solution.py:78
  51.1 1.0 copy-start.2
  59.4 34.3 %all-to-all-start.2 = ((f32[96,128,16]{0,2,1:T(8,128)}), f32[96,128,16]{0,2,1:T(8,128)}, u32[]{:S(2)}, u32[]{:S(2)}) async-start(f32[96,128,16]{0,2,1:T(8,128)} %copy.152), calls=%async_computation.2 | async-start | bytes 2097152 | tf_op jit(solution)/shard_map/all_to_all | solution.py:100
  93.7 34.9 %all-to-all-start.1 = ((f32[96,128,16]{0,2,1:T(8,128)}), f32[96,128,16]{0,2,1:T(8,128)}, u32[]{:S(2)}, u32[]{:S(2)}) async-start(f32[96,128,16]{0,2,1:T(8,128)} %copy.150), calls=%async_computation.1 | async-start | bytes 2097152 | tf_op jit(solution)/shard_map/all_to_all | solution.py:99
  128.5 3.0 copy-start.3
  163.5 34.9 %all-to-all-start.3 = ((f32[96,2,1024]{0,1,2:T(2,128)}), f32[96,2,1024]{0,1,2:T(2,128)}, u32[]{:S(2)}, u32[]{:S(2)}) async-start(f32[96,2,1024]{0,1,2:T(2,128)} %copy.166), calls=%async_computation.3 | async-start | bytes 2097152 | tf_op jit(solution)/shard_map/all_to_all | solution.py:146
  198.4 34.9 %all-to-all-start.4 = ((f32[96,2,1024]{0,1,2:T(2,128)}), f32[96,2,1024]{0,1,2:T(2,128)}, u32[]{:S(2)}, u32[]{:S(2)}) async-start(f32[96,2,1024]{0,1,2:T(2,128)} %copy.170), calls=%async_computation.4 | async-start | bytes 2097152 | tf_op jit(solution)/shard_map/all_to_all | solution.py:147
  234.5 1.0 copy-start.4
  238.8 13.1 %copy-start.8 = (f32[64,32]{0,1:T(8,128)S(1)}, f32[64,32]{0,1:T(8,128)}, u32[]{:S(2)}) copy-start(f32[64,32]{0,1:T(8,128)} %param.10) | copy-start | bytes 24580
  240.9 13.2 %copy-start.11 = (s32[32]{0:T(128)S(1)}, s32[32]{0:T(128)}, u32[]{:S(2)}) copy-start(s32[32]{0:T(128)} %copy-done.10) | copy-start | bytes 388
  240.9 13.2 %copy-start.13 = (pred[32]{0:T(512)(128)(4,1)S(1)}, pred[32]{0:T(512)(128)(4,1)}, u32[]{:S(2)}) copy-start(pred[32]{0:T(512)(128)(4,1)} %copy-done.12) | copy-start | bytes 100
  240.9 93.6 %all-to-all-start.5 = ((f32[64,1,1024]{2,1,0:T(1,128)}), f32[64,1,1024]{2,1,0:T(1,128)}, u32[]{:S(2)}, u32[]{:S(2)}) async-start(f32[64,1,1024]{2,1,0:T(1,128)} %reshape.322), calls=%async_computation.5 | async-start | bytes 524288 | tf_op jit(solution)/shard_map/all_to_all | solution.py:155
  341.0 3.1 collective-permute-start.1
  344.1 253.9 %copy-start.1 = (f32[32,64]{1,0:T(8,128)S(1)}, f32[32,64]{1,0:T(8,128)}, u32[]{:S(2)}) copy-start(f32[32,64]{1,0:T(8,128)} %param.9) | copy-start | bytes 24580
where the time goes:
time: 605 us; the launch traced here: 599 us
  blocking collectives  326 us (54%)
  waiting for transfers between devices  106 us (18%)
  matrix products  52.9 us (9%)
  starting transfers between devices  50.4 us (8%)
  local copies, waits for them, and re-layouts  42.8 us (7%)
  other arithmetic  18.9 us (3%)
    psum x1, blocking collectives, shards(): short_total, out_total = lax.psum((short_part, out_part), 'seq')  250 us
    psum x1, blocking collectives, shards(): in_total = lax.psum(in_part, ('seq', 'ch'))  75.9 us
    all_to_all x1, waiting for transfers between devices, shards(): lax.all_to_all(turned_imag, 'seq', split_axis=1, concat_axis=2, tiled=True)  25.5 us
    all_to_all x1, waiting for transfers between devices, shards(): lax.all_to_all(part_real, 'seq', split_axis=2, concat_axis=1, tiled=True)  25 us
    all_to_all x1, waiting for transfers between devices, shards(): lax.all_to_all(part_imag, 'seq', split_axis=2, concat_axis=1, tiled=True)  24.7 us
    all_to_all x1, waiting for transfers between devices, shards(): lax.all_to_all(turned_real, 'seq', split_axis=1, concat_axis=2, tiled=True)  23.3 us
    all_to_all x1, starting transfers between devices, shards(): lax.all_to_all(both_signals, 'seq', split_axis=2, concat_axis=1, tiled=True)  13.3 us
    unnamed x38, local copies, waits for them, and re-layouts  12.3 us
  transfers between devices with their start and end apart: 8, of which 6 were waited for; matrix products, arithmetic and copies ran while one was open for 6% of the time, Pallas kernels for 0%

commit v1 on v0

--- a/solution.py
+++ b/solution.py
@@ -178,7 +178,7 @@
         )
     grad_proj = result.astype(jnp.bfloat16)
     short_total, out_total = lax.psum((short_part, out_part), "seq")
-    in_total = lax.psum(in_part, ("seq", "ch"))
+    in_total = jnp.sum(lax.all_gather(in_part, ("seq", "ch")), axis=0)
     return (grad_proj, short_total * norm_scale, out_total * norm_scale, in_total * norm_scale)
 
 

time: 605 us -> 555 us (0.917)
  blocking collectives: 326 us -> 268 us
  between operations: 1.66 us -> 15.1 us
  starting transfers between devices: 50.4 us -> 43.8 us
    psum x1 -> x0, blocking collectives: 75.9 us -> none  [shards(): in_total = lax.psum(in_part, ('seq', 'ch'))]
    all_to_all x0 -> x1, blocking collectives: none -> 18.8 us  [shards(): lax.all_to_all(jnp.concatenate([conv_cols, gated_cols], 0), 'seq', split_...]
    all_to_all x1 -> x0, starting transfers between devices: 6.96 us -> none  [shards(): lax.all_to_all(jnp.concatenate([conv_cols, gated_cols], 0), 'seq', split_...]
    unnamed x38 -> x44, local copies, waits for them, and re-layouts: 12.3 us -> 13.2 us
  transfers between devices with their start and end apart: 8 -> 8, of which waited for: 6 -> 6; matrix products, arithmetic and copies ran while one was open for 6% -> 7% of each run, Pallas kernels for 0% -> 0%
where the time goes in v1:
time: 555 us; the launch traced here: 548 us
  blocking collectives  268 us (48%)
  waiting for transfers between devices  105 us (19%)
  matrix products  52.4 us (9%)
  starting transfers between devices  43.8 us (8%)
  local copies, waits for them, and re-layouts  42.8 us (8%)
  other arithmetic  21.5 us (4%)
  between operations  15.1 us (3%)
    psum x1, blocking collectives, shards(): short_total, out_total = lax.psum((short_part, out_part), 'seq')  249 us
    all_to_all x1, waiting for transfers between devices, shards(): lax.all_to_all(turned_imag, 'seq', split_axis=1, concat_axis=2, tiled=True)  25.5 us
    all_to_all x1, waiting for transfers between devices, shards(): lax.all_to_all(part_real, 'seq', split_axis=2, concat_axis=1, tiled=True)  25 us
    all_to_all x1, waiting for transfers between devices, shards(): lax.all_to_all(part_imag, 'seq', split_axis=2, concat_axis=1, tiled=True)  24.4 us
    all_to_all x1, waiting for transfers between devices, shards(): lax.all_to_all(turned_real, 'seq', split_axis=1, concat_axis=2, tiled=True)  23.3 us
    all_to_all x1, blocking collectives, shards(): lax.all_to_all(jnp.concatenate([conv_cols, gated_cols], 0), 'seq', split_...  18.8 us
    all_to_all x1, starting transfers between devices, shards(): lax.all_to_all(both_signals, 'seq', split_axis=2, concat_axis=1, tiled=True)  13.3 us
    unnamed x44, local copies, waits for them, and re-layouts  13.2 us
  transfers between devices with their start and end apart: 8, of which 6 were waited for; matrix products, arithmetic and copies ran while one was open for 7% of the time, Pallas kernels for 0%

profile of v1, /device:TPU:8, one launch (start us, length us, event | category | flops | bytes accessed | tf_op | source)
XLA Modules:
  0.0 548.4 jit_solution(8592697006358385771)
XLA Ops:
  8.0 1.7 collective-permute-start
  10.9 5.1 fusion.244
  19.0 3.8 reduce
  22.8 2.1 reshape.321
  24.9 13.3 %all-to-all-start = ((f32[64,1,1024]{2,1,0:T(1,128)}), f32[64,1,1024]{2,1,0:T(1,128)}, u32[]{:S(2)}, u32[]{:S(2)}) async-start(f32[64,1,1024]{2,1,0:T(1,128)} %reshape.321), calls=%async_computation | async-start | bytes 524288 | tf_op jit(solution)/shard_map/all_to_all | solution.py:78
  38.2 1.9 fusion.11
  40.1 1.9 copy.146
  42.1 2.0 copy.148
  44.2 5.8 %all-to-all-done = f32[64,1,1024]{2,1,0:T(1,128)} async-done(((f32[64,1,1024]{2,1,0:T(1,128)}), f32[64,1,1024]{2,1,0:T(1,128)}, u32[]{:S(2)}, u32[]{:S(2)}) %all-to-all-start) | async-done | bytes 262176 | tf_op jit(solution)/shard_map/all_to_all | solution.py:78
  50.0 2.9 reduce.1
  53.0 2.5 reshape.322
  55.4 2.3 fusion.241
  58.8 1.7 convolution_negate_fusion
  60.6 2.9 add_bitcast_fusion.1
  63.4 2.5 copy.152
  65.9 6.3 %all-to-all-start.2 = ((f32[96,128,16]{0,2,1:T(8,128)}), f32[96,128,16]{0,2,1:T(8,128)}, u32[]{:S(2)}, u32[]{:S(2)}) async-start(f32[96,128,16]{0,2,1:T(8,128)} %copy.152), calls=%async_computation.2 | async-start | bytes 2097152 | tf_op jit(solution)/shard_map/all_to_all | solution.py:100
  72.2 2.5 copy.150
  74.7 25.5 %all-to-all-done.2 = f32[96,128,16]{0,2,1:T(8,128)} async-done(((f32[96,128,16]{0,2,1:T(8,128)}), f32[96,128,16]{0,2,1:T(8,128)}, u32[]{:S(2)}, u32[]{:S(2)}) %all-to-all-start.2) | async-done | bytes 786464 | tf_op jit(solution)/shard_map/all_to_all | solution.py:100
  100.2 7.2 %all-to-all-start.1 = ((f32[96,128,16]{0,2,1:T(8,128)}), f32[96,128,16]{0,2,1:T(8,128)}, u32[]{:S(2)}, u32[]{:S(2)}) async-start(f32[96,128,16]{0,2,1:T(8,128)} %copy.150), calls=%async_computation.1 | async-start | bytes 2097152 | tf_op jit(solution)/shard_map/all_to_all | solution.py:99
  108.0 3.8 fusion.14
  111.8 23.3 %all-to-all-done.1 = f32[96,128,16]{0,2,1:T(8,128)} async-done(((f32[96,128,16]{0,2,1:T(8,128)}), f32[96,128,16]{0,2,1:T(8,128)}, u32[]{:S(2)}, u32[]{:S(2)}) %all-to-all-start.1) | async-done | bytes 786464 | tf_op jit(solution)/shard_map/all_to_all | solution.py:99
  135.1 2.9 fusion.18
  138.0 2.9 fusion.7
  140.9 3.4 subtract_bitcast_fusion
  144.3 1.6 fusion.29
  146.0 1.6 fusion.33
  147.6 1.7 fusion.5
  149.3 1.8 fusion.6
  157.7 1.9 multiply_subtract_fusion
  161.0 1.6 fusion.27
  166.6 1.7 fusion.13
  168.2 1.8 copy.166
  170.0 6.8 %all-to-all-start.3 = ((f32[96,2,1024]{0,1,2:T(2,128)}), f32[96,2,1024]{0,1,2:T(2,128)}, u32[]{:S(2)}, u32[]{:S(2)}) async-start(f32[96,2,1024]{0,1,2:T(2,128)} %copy.166), calls=%async_computation.3 | async-start | bytes 2097152 | tf_op jit(solution)/shard_map/all_to_all | solution.py:146
  176.8 3.0 copy.170
  179.9 25.0 %all-to-all-done.3 = f32[96,2,1024]{0,1,2:T(2,128)} async-done(((f32[96,2,1024]{0,1,2:T(2,128)}), f32[96,2,1024]{0,1,2:T(2,128)}, u32[]{:S(2)}, u32[]{:S(2)}) %all-to-all-start.3) | async-done | bytes 786464 | tf_op jit(solution)/shard_map/all_to_all | solution.py:146
  204.9 6.8 %all-to-all-start.4 = ((f32[96,2,1024]{0,1,2:T(2,128)}), f32[96,2,1024]{0,1,2:T(2,128)}, u32[]{:S(2)}, u32[]{:S(2)}) async-start(f32[96,2,1024]{0,1,2:T(2,128)} %copy.170), calls=%async_computation.4 | async-start | bytes 2097152 | tf_op jit(solution)/shard_map/all_to_all | solution.py:147
  213.4 1.8 fusion.21
  215.3 24.4 %all-to-all-done.4 = f32[96,2,1024]{0,1,2:T(2,128)} async-done(((f32[96,2,1024]{0,1,2:T(2,128)}), f32[96,2,1024]{0,1,2:T(2,128)}, u32[]{:S(2)}, u32[]{:S(2)}) %all-to-all-start.4) | async-done | bytes 786464 | tf_op jit(solution)/shard_map/all_to_all | solution.py:147
  245.3 1.9 copy.176
  247.1 2.2 convolution_multiply_fusion.4
  249.4 3.6 fusion.43
  253.1 2.1 copy.229
  255.2 2.1 reshape.323
  257.3 18.8 %all_to_all.84 = f32[64,1,1024]{2,1,0:T(1,128)} all-to-all(f32[64,1,1024]{2,1,0:T(1,128)} %reshape.323), channel_id=1, replica_groups=mesh['seq'=64,'ch'=4] {'seq'}, dimensions={0} | all-to-all | bytes 524288 | tf_op jit(solution)/shard_map/all_to_all | solution.py:155
  276.0 2.9 reduce.2
  279.0 1.9 reshape.324
  288.0 248.8 %all-reduce = (f32[3,32,3]{1,0,2:T(4,128)S(1)}, f32[64,32]{0,1:T(8,128)S(1)}) all-reduce(f32[3,32,3]{1,0,2:T(4,128)S(1)} %pad_maximum_fusion.7, f32[64,32]{0,1:T(8,128)S(1)} %fusion.238), channel_id=1, replica_groups=mesh['seq'=64,'ch'=4] {'seq'}, use_global_device_ids=true, to_apply=%region_3.4 | all-reduce | flops 2336 | bytes 18688 | tf_op jit(solution)/shard_map/psum | solution.py:180
  538.0 2.5 reduce_sum.39
  (102 shorter events, 34.6 us)
Async XLA Ops:
  7.2 3.7 copy-start
  7.2 8.8 %copy-start.8 = (bf16[32,1024]{1,0:T(8,128)(2,1)S(1)}, bf16[32,1024]{1,0:T(8,128)(2,1)}, u32[]{:S(2)}) copy-start(bf16[32,1024]{1,0:T(8,128)(2,1)} %param.7) | copy-start | bytes 196612
  8.0 8.1 %collective-permute-start = (bf16[3,32,2]{2,1,0:T(8,128)(2,1)S(1)}, bf16[3,32,2]{2,1,0:T(8,128)(2,1)S(1)}, u32[]{:S(2)}, u32[]{:S(2)}) collective-permute-start(bf16[3,32,2]{2,1,0:T(8,128)(2,1)S(1)} %slice.96), channel_id=1, source_target_pairs={{0,4},{4,8},{8,12},{12,16},{16,20},{20,24},{24,28},{28,32},{32,36}... | collective-permute-start | bytes 1160 | tf_op jit(solution)/shard_map/ppermute | solution.py:13
  9.8 6.3 %copy-start.12 = (s32[32]{0:T(128)}, s32[32]{0:T(128)S(1)}, u32[]{:S(2)}) copy-start(s32[32]{0:T(128)S(1)} %get-tuple-element.66) | copy-start | bytes 388
  9.8 6.3 %copy-start.14 = (pred[32]{0:T(512)(128)(4,1)}, pred[32]{0:T(512)(128)(4,1)S(1)}, u32[]{:S(2)}) copy-start(pred[32]{0:T(512)(128)(4,1)S(1)} %fusion.143) | copy-start | bytes 100
  10.9 5.3 copy-start.6
  18.5 19.7 %copy-start.11 = (f32[32]{0:T(128)S(1)}, f32[32]{0:T(128)}, u32[]{:S(2)}) copy-start(f32[32]{0:T(128)} %param.11) | copy-start | bytes 388
  18.5 19.7 %copy-start.9 = (f32[64,32]{0,1:T(8,128)S(1)}, f32[64,32]{0,1:T(8,128)}, u32[]{:S(2)}) copy-start(f32[64,32]{0,1:T(8,128)} %param.10) | copy-start | bytes 24580
  24.9 25.2 %all-to-all-start = ((f32[64,1,1024]{2,1,0:T(1,128)}), f32[64,1,1024]{2,1,0:T(1,128)}, u32[]{:S(2)}, u32[]{:S(2)}) async-start(f32[64,1,1024]{2,1,0:T(1,128)} %reshape.321), calls=%async_computation | async-start | bytes 524288 | tf_op jit(solution)/shard_map/all_to_all | solution.py:78
  57.8 1.0 copy-start.2
  65.9 34.3 %all-to-all-start.2 = ((f32[96,128,16]{0,2,1:T(8,128)}), f32[96,128,16]{0,2,1:T(8,128)}, u32[]{:S(2)}, u32[]{:S(2)}) async-start(f32[96,128,16]{0,2,1:T(8,128)} %copy.152), calls=%async_computation.2 | async-start | bytes 2097152 | tf_op jit(solution)/shard_map/all_to_all | solution.py:100
  100.2 34.9 %all-to-all-start.1 = ((f32[96,128,16]{0,2,1:T(8,128)}), f32[96,128,16]{0,2,1:T(8,128)}, u32[]{:S(2)}, u32[]{:S(2)}) async-start(f32[96,128,16]{0,2,1:T(8,128)} %copy.150), calls=%async_computation.1 | async-start | bytes 2097152 | tf_op jit(solution)/shard_map/all_to_all | solution.py:99
  135.1 2.9 copy-start.4
  170.0 34.9 %all-to-all-start.3 = ((f32[96,2,1024]{0,1,2:T(2,128)}), f32[96,2,1024]{0,1,2:T(2,128)}, u32[]{:S(2)}, u32[]{:S(2)}) async-start(f32[96,2,1024]{0,1,2:T(2,128)} %copy.166), calls=%async_computation.3 | async-start | bytes 2097152 | tf_op jit(solution)/shard_map/all_to_all | solution.py:146
  204.9 34.9 %all-to-all-start.4 = ((f32[96,2,1024]{0,1,2:T(2,128)}), f32[96,2,1024]{0,1,2:T(2,128)}, u32[]{:S(2)}, u32[]{:S(2)}) async-start(f32[96,2,1024]{0,1,2:T(2,128)} %copy.170), calls=%async_computation.4 | async-start | bytes 2097152 | tf_op jit(solution)/shard_map/all_to_all | solution.py:147
  211.7 326.3 %all-gather.3.cloned.1.call-start = ((), (), s32[]{:S(2)}) async-start(), calls=%async_computation.6 | async-start | bytes 4210688 | tf_op jit(solution)/shard_map/all_gather | solution.py:181
  241.0 1.0 copy-start.5
  243.1 0.8 copy-start.3
  243.9 3.2 copy-start.10
  243.9 5.4 copy-start.13
  243.9 5.4 copy-start.15
  282.5 1.4 copy-start.7
  282.5 1.4 copy-start.16
  282.6 3.1 collective-permute-start.1
  538.0 3.2 copy-start.1
Sparse Core Ops, SparseCore 0:
  253.2 112.9 all-gather.2
